TPU v7x, 32 devices: a whole 2x2x4 slice. The times are simulated.
32 devices in a mesh: section: 4 (over z), dp: 4 (over y, x), hid: 2 (over core).
Axes of the slice: x: 2, y: 2, z: 4, core: 2. Of those that a mesh axis runs over, the one named last changes fastest.
Arguments:
- forward_input: bfloat16 [4, 768, 2048], P('section', 'dp'), may hold values from -6 to 6
- backward_input: bfloat16 [4, 768, 2048], P('section', 'dp'), may hold values from -6 to 6
- output_grad: bfloat16 [4, 768, 2048], P('section', 'dp'), may hold values from -8 to 8
- norm_gain: float32 [4, 2048], P('section'), may hold values from 0.5 to 1.5
- in_weight: float32 [4, 2, 2048, 512], P('section', None, 'dp', 'hid'), may hold values from -0.125 to 0.125
- out_weight: float32 [4, 512, 2048], P('section', 'hid', 'dp'), may hold values from -0.25 to 0.25
- in_codes: int32 [4, 2, 2048, 512], P('section', None, 'dp', 'hid'), may hold values from 0 to 32511
- out_codes: int32 [4, 512, 2048], P('section', 'hid', 'dp'), may hold values from 0 to 32511
- in_scales: float32 [4, 2, 2, 2048, 2], P('section', None, None, 'dp', 'hid'), may hold values from 0.005 to 0.05
- out_scales: float32 [4, 2, 2, 2048], P('section', None, 'hid', 'dp'), may hold values from 0.005 to 0.05
- section_lags: int32 [4], P('section'), may hold values from 1 to 4
Outputs:
- next_input: bfloat16 [4, 768, 2048], P('section', 'dp')
- input_grad: bfloat16 [4, 768, 2048], P('section', 'dp')
- in_update: float32 [4, 2, 2048, 512], P('section', None, 'dp', 'hid')
- out_update: float32 [4, 512, 2048], P('section', 'hid', 'dp')
Inputs may be any that keep to these rules, and one draw needn't show every extreme that they name: `in_codes`: each code holds a first-moment code of 0 to 126 times 256 plus a second-moment code of 0 to 255. `out_codes`: each code holds a first-moment code of 0 to 126 times 256 plus a second-moment code of 0 to 255.
All inputs are finite; a program needn't handle non-finite values.
Results may differ from a plain program's by a relative error of at most 0.012.
Values may be sent and summed in bfloat16 or wider, within the bound.
A program may use at most 64 MiB of HBM per device.

v0:
```python
import jax
import jax.numpy as jnp
from jax import lax
from jax.sharding import PartitionSpec as P

QB = 256
STEP = 1000
BETA_ONE = 0.9
BETA_TWO = 0.999
ADAM_EPS = 1e-08
NORM_EPS = 1e-06
LEARN_RATE = 0.003


def passed_along(block, axis, distance):
    devices = range(lax.axis_size(axis))
    route = [(i - distance, i) for i in devices if i - distance in devices]
    return lax.ppermute(block, axis, route)


def dequant(codes, first_scale, second_scale):
    high = (codes // 256).astype(jnp.float32)
    low = (codes % 256).astype(jnp.float32)
    moment_m = first_scale * (high - 63.0) / 63.0
    moment_v = jnp.square(second_scale * (0.25 + 0.75 * low / 255.0))
    return (moment_m, moment_v)


def direction(moment_m, moment_v, count):
    return (
        moment_m
        / (1.0 - BETA_ONE**count)
        / (jnp.sqrt(moment_v / (1.0 - BETA_TWO**count)) + ADAM_EPS)
    )


def normalize(inputs, gain):
    values = inputs.astype(jnp.float32)
    factor = lax.rsqrt(jnp.mean(values * values, axis=-1, keepdims=True) + NORM_EPS)
    return ((values * factor * gain).astype(jnp.bfloat16), factor, values)


def local(
    forward_input,
    backward_input,
    output_grad,
    norm_gain,
    in_weight,
    out_weight,
    in_codes,
    out_codes,
    in_scales,
    out_scales,
    section_lags,
):
    lag_value = section_lags[0].astype(jnp.float32)
    gain = norm_gain[0]
    m_in, v_in = dequant(
        in_codes[0],
        jnp.repeat(in_scales[0, 0], QB, axis=-1),
        jnp.repeat(in_scales[0, 1], QB, axis=-1),
    )
    m_out, v_out = dequant(
        out_codes[0],
        jnp.repeat(out_scales[0, 0], QB, axis=0),
        jnp.repeat(out_scales[0, 1], QB, axis=0),
    )
    pred_in = (in_weight[0] - LEARN_RATE * lag_value * direction(m_in, v_in, STEP - 1)).astype(
        jnp.bfloat16
    )
    pred_out = (out_weight[0] - LEARN_RATE * lag_value * direction(m_out, v_out, STEP - 1)).astype(
        jnp.bfloat16
    )
    full_in, full_out = (
        lax.all_gather(pred_in, "dp", axis=1, tiled=True),
        lax.all_gather(pred_out, "dp", axis=1, tiled=True),
    )
    normed, factor, values = normalize(forward_input[0], gain)
    gate_val = jnp.dot(normed, full_in[0], preferred_element_type=jnp.float32)
    up_val = jnp.dot(normed, full_in[1], preferred_element_type=jnp.float32)
    hidden = (gate_val * jax.nn.sigmoid(gate_val) * up_val).astype(jnp.bfloat16)
    partial_value = jnp.dot(hidden, full_out, preferred_element_type=jnp.float32)
    back_in, back_out = (full_in, full_out)
    out_cot = output_grad[0]
    normed_b, factor_b, values_b = normalize(backward_input[0], gain)
    gate_b = jnp.dot(normed_b, back_in[0], preferred_element_type=jnp.float32)
    up_b = jnp.dot(normed_b, back_in[1], preferred_element_type=jnp.float32)
    sig_b = jax.nn.sigmoid(gate_b)
    hidden_b = (gate_b * sig_b * up_b).astype(jnp.bfloat16)
    grad_h = jnp.dot(out_cot, back_out.T, preferred_element_type=jnp.float32)
    grad_gate = (grad_h * up_b * sig_b * (1.0 + gate_b * (1.0 - sig_b))).astype(jnp.bfloat16)
    grad_up = (grad_h * gate_b * sig_b).astype(jnp.bfloat16)
    grad_part = jnp.dot(grad_gate, back_in[0].T, preferred_element_type=jnp.float32) + jnp.dot(
        grad_up, back_in[1].T, preferred_element_type=jnp.float32
    )
    summed, grad_n = (
        lax.psum(partial_value.astype(jnp.bfloat16), "hid").astype(jnp.float32),
        lax.psum(grad_part.astype(jnp.bfloat16), "hid").astype(jnp.float32),
    )
    ahead = (values + summed).astype(jnp.bfloat16)
    next_rows = passed_along(ahead, "section", 1)
    scaled = gain * grad_n
    grad_x = (
        out_cot.astype(jnp.float32)
        + factor_b * scaled
        - values_b * factor_b**3 * jnp.mean(scaled * values_b, axis=-1, keepdims=True)
    )
    back_rows = passed_along(grad_x.astype(jnp.bfloat16), "section", -1)
    local_in = jnp.stack(
        [
            jnp.dot(normed_b.T, grad_gate, preferred_element_type=jnp.float32),
            jnp.dot(normed_b.T, grad_up, preferred_element_type=jnp.float32),
        ]
    )
    local_out = jnp.dot(hidden_b.T, out_cot, preferred_element_type=jnp.float32)
    sum_in, sum_out = (
        lax.psum_scatter(
            local_in.astype(jnp.bfloat16), "dp", scatter_dimension=1, tiled=True
        ).astype(jnp.float32),
        lax.psum_scatter(
            local_out.astype(jnp.bfloat16), "dp", scatter_dimension=1, tiled=True
        ).astype(jnp.float32),
    )
    rows_all = out_cot.shape[0] * lax.axis_size("dp")
    grad_in = sum_in / rows_all
    grad_out = sum_out / rows_all
    new_m_in = BETA_ONE * m_in + (1.0 - BETA_ONE) * grad_in
    new_v_in = BETA_TWO * v_in + (1.0 - BETA_TWO) * grad_in * grad_in
    new_m_out = BETA_ONE * m_out + (1.0 - BETA_ONE) * grad_out
    new_v_out = BETA_TWO * v_out + (1.0 - BETA_TWO) * grad_out * grad_out
    in_update = direction(new_m_in, new_v_in, STEP)
    out_update = direction(new_m_out, new_v_out, STEP)
    return (next_rows[None], back_rows[None], in_update[None], out_update[None])


def solution(mesh):
    in_specs = (
        P("section", "dp", None),
        P("section", "dp", None),
        P("section", "dp", None),
        P("section", None),
        P("section", None, "dp", "hid"),
        P("section", "hid", "dp"),
        P("section", None, "dp", "hid"),
        P("section", "hid", "dp"),
        P("section", None, None, "dp", "hid"),
        P("section", None, "hid", "dp"),
        P("section"),
    )
    out_specs = (
        P("section", "dp", None),
        P("section", "dp", None),
        P("section", None, "dp", "hid"),
        P("section", "hid", "dp"),
    )
    return jax.shard_map(local, mesh=mesh, in_specs=in_specs, out_specs=out_specs, check_vma=False)
```

profile of v0, /device:TPU:0, one launch (start us, length us, event | category | flops | bytes accessed | tf_op | source)
XLA Modules:
  0.0 193.6 jit_solution(17537712004479626247)
XLA Ops:
  7.2 0.0 all-gather.3.cloned.1.call-start
  7.9 0.7 fusion.87
  8.6 0.0 copy-start.13
  8.6 4.1 %fusion.40 = bf16[2,512,256]{2,1,0:T(8,128)(2,1)} fusion(f32[1,2,512,256]{3,2,1,0:T(8,128)} %param.15, f32[]{:T(128)} %bitcast.4, s32[1,2,512,256]{3,2,1,0:T(8,128)} %param.17, f32[2,512]{1,0:T(2,128)S(1)} %get-tuple-element.17, f32[2,512]{1,0:T(2,128)S(1)} %get-tuple-element.16), kind=kLoop, calls=%fused_computation.66 | loop fusion | flops 8912896 | bytes 2629636 | tf_op jit(solution)/shard_map/convert_element_type | solution.py:68
  12.7 0.0 all-gather.3.cloned.1.call-update
  12.7 0.0 reduce-scatter.5.cloned.1.call-start
  12.8 0.2 fusion.13
  13.0 37.7 %all-gather.3.cloned.1.call-done = bf16[2,2048,256]{2,1,0:T(8,128)(2,1)} async-done(((bf16[2,512,256]{2,1,0:T(8,128)(2,1)}), bf16[2,2048,256]{2,1,0:T(8,128)(2,1)}) %all-gather.3.cloned.1.call-update) | async-done | bytes 2097168 | tf_op jit(solution)/shard_map/all_gather | solution.py:75
  50.8 0.0 copy-done.13
  50.8 1.8 fusion.45
  52.6 0.1 copy-done.5
  52.7 0.4 fusion.43
  53.1 0.8 copy-done.3
  53.9 1.5 convolution_convert_fusion
  55.4 0.0 copy-done.9
  55.4 0.0 reduce-scatter.5.cloned.1.call-update
  55.4 0.0 all-gather.5.cloned.1.call-start
  55.5 28.0 %reduce-scatter.5.cloned.1.call-done = bf16[256,512]{1,0:T(8,128)(2,1)} async-done(((bf16[256,2048]{1,0:T(8,128)(2,1)}), bf16[256,512]{1,0:T(8,128)(2,1)}) %reduce-scatter.5.cloned.1.call-update) | async-done | bytes 262160 | tf_op jit(solution)/shard_map/reduce_scatter | solution.py:120
  83.5 3.0 %fusion.61 = (f32[1,256,512]{2,1,0:T(8,128)}, bf16[256,512]{1,0:T(8,128)(2,1)}) fusion(bf16[256,512]{1,0:T(8,128)(2,1)} %reduce-scatter.5.cloned.1.call-done, s32[1,256,512]{2,1,0:T(8,128)S(1)} %copy-done.7, f32[512]{0:T(512)S(1)} %bitcast.177, f32[512]{0:T(512)S(1)} %bitcast.176, f32[]{:T(128)} %bitcast.4, f32[1,256,512]{2,1,0:T(8,128)S(1)} %copy-done.8), kind=kLoop, calls=%fused_computation.95 | loop fusion | flops 6029312 | bytes 2101252 | tf_op jit(solution)/shard_map/broadcast_in_dim | solution.py:133
  86.5 0.0 all-gather.5.cloned.1.call-update
  86.5 0.0 all-reduce.3.cloned.1.call-start
  86.6 0.2 fusion.9
  86.8 0.0 copy-start.12
  86.8 1.7 fusion.44
  88.6 24.5 %all-gather.5.cloned.1.call-done = bf16[256,2048]{1,0:T(8,128)(2,1)} async-done(((bf16[256,512]{1,0:T(8,128)(2,1)}), bf16[256,2048]{1,0:T(8,128)(2,1)}) %all-gather.5.cloned.1.call-update) | async-done | bytes 1048592 | tf_op jit(solution)/shard_map/all_gather | solution.py:76
  113.0 1.7 multiply_convert_fusion.1
  114.8 3.5 %convolution_convert_fusion.3 = bf16[192,2048]{1,0:T(8,128)(2,1)} fusion(bf16[256,2048]{1,0:T(8,128)(2,1)} %all-gather.5.cloned.1.call-done, bf16[2,2048,256]{2,1,0:T(8,128)(2,1)} %all-gather.3.cloned.1.call-done, bf16[1,192,2048]{2,1,0:T(8,128)(2,1)S(1)} %copy-done.2, f32[2048]{0:T(1024)S(1)} %bitcast.171, f32[192]{0:T(256)S(1)} %add_rsqrt_fusion.1, ...), kind=kOutput, calls=%fused_computation.5 | convolution fusion | flops 404914176 | bytes 3875584 | tf_op jit(solution)/shard_map/dot_general | solution.py:82
  118.3 1.9 fusion.42
  120.2 0.0 copy-done.6
  120.2 1.4 fusion
  121.6 0.0 all-reduce.3.cloned.1.call-update
  121.6 0.0 reduce-scatter.3.cloned.1.call-start
  121.7 0.6 fusion.2
  122.3 0.6 fusion.1
  122.8 1.5 pad_maximum_fusion
  124.3 0.0 reduce-scatter.3.cloned.1.call-update
  124.4 17.8 %all-reduce.3.cloned.1.call-done = (bf16[192,2048]{1,0:T(8,128)(2,1)}, bf16[192,2048]{1,0:T(8,128)(2,1)}) async-done(((bf16[192,2048]{1,0:T(8,128)(2,1)}, bf16[192,2048]{1,0:T(8,128)(2,1)}), (bf16[192,2048]{1,0:T(8,128)(2,1)}, bf16[192,2048]{1,0:T(8,128)(2,1)})) %all-reduce.3.cloned.1.call-update) | async-done | bytes 1572880 | tf_op jit(solution)/shard_map/psum | solution.py:97
  142.2 1.5 fusion.10
  143.7 3.7 %collective-permute-start = (bf16[192,2048]{1,0:T(8,128)(2,1)S(1)}, bf16[192,2048]{1,0:T(8,128)(2,1)S(1)}, u32[]{:S(2)}, u32[]{:S(2)}) collective-permute-start(bf16[192,2048]{1,0:T(8,128)(2,1)S(1)} %fusion.10), channel_id=1, source_target_pairs={{0,8},{8,16},{16,24},{1,9},{9,17},{17,25},{2,10},{10,18},{18,26},{... | collective-permute-start | bytes 2359304 | tf_op jit(solution)/shard_map/ppermute | solution.py:18
  147.4 0.3 fusion.17
  147.8 0.6 fusion.16
  148.4 1.3 collective-permute-start.1
  149.7 14.9 %collective-permute-done = bf16[192,2048]{1,0:T(8,128)(2,1)S(1)} collective-permute-done((bf16[192,2048]{1,0:T(8,128)(2,1)S(1)}, bf16[192,2048]{1,0:T(8,128)(2,1)S(1)}, u32[]{:S(2)}, u32[]{:S(2)}) %collective-permute-start) | collective-permute-done | bytes 786464 | tf_op jit(solution)/shard_map/ppermute | solution.py:18
  164.6 5.1 %collective-permute-done.1 = bf16[192,2048]{1,0:T(8,128)(2,1)S(1)} collective-permute-done((bf16[192,2048]{1,0:T(8,128)(2,1)S(1)}, bf16[192,2048]{1,0:T(8,128)(2,1)S(1)}, u32[]{:S(2)}, u32[]{:S(2)}) %collective-permute-start.1) | collective-permute-done | bytes 786464 | tf_op jit(solution)/shard_map/ppermute | solution.py:18
  169.7 11.7 %reduce-scatter.3.cloned.1.call-done = bf16[2,512,256]{2,1,0:T(8,128)(2,1)} async-done(((bf16[2,2048,256]{2,1,0:T(8,128)(2,1)}), bf16[2,512,256]{2,1,0:T(8,128)(2,1)}) %reduce-scatter.3.cloned.1.call-update) | async-done | bytes 524304 | tf_op jit(solution)/shard_map/reduce_scatter | solution.py:117
  181.4 3.9 %fusion.33 = f32[1,2,512,256]{3,2,1,0:T(8,128)} fusion(bf16[2,512,256]{2,1,0:T(8,128)(2,1)} %reduce-scatter.3.cloned.1.call-done, s32[1,2,512,256]{3,2,1,0:T(8,128)S(1)} %copy-done.1, f32[2,512]{1,0:T(2,128)S(1)} %get-tuple-element.17, f32[2,512]{1,0:T(2,128)S(1)} %get-tuple-element.16), kind=kLoop, calls=%fused_computation.54 | loop fusion | flops 10223616 | bytes 2629632 | tf_op jit(solution)/shard_map/broadcast_in_dim | solution.py:133
  185.3 0.9 copy.24
  186.2 0.9 copy.25
  (28 shorter events, 0.1 us)
Async XLA Ops:
  7.2 43.6 %all-gather.3.cloned.1.call-start = ((), (), s32[]{:S(2)}) async-start(), calls=%async_computation.2 | async-start | bytes 2621440 | tf_op jit(solution)/shard_map/all_gather | solution.py:75
  8.6 4.2 %copy-start = (bf16[1,192,2048]{2,1,0:T(8,128)(2,1)S(1)}, bf16[1,192,2048]{2,1,0:T(8,128)(2,1)}, u32[]{:S(2)}) copy-start(bf16[1,192,2048]{2,1,0:T(8,128)(2,1)} %param.12) | copy-start | bytes 2359300
  8.6 42.2 %copy-start.13 = (f32[1,2048]{1,0:T(1,128)S(1)}, f32[1,2048]{1,0:T(1,128)}, u32[]{:S(2)}) copy-start(f32[1,2048]{1,0:T(1,128)} %param.14) | copy-start | bytes 24580
  12.7 70.8 %reduce-scatter.5.cloned.1.call-start = ((), (), s32[]{:S(2)}) async-start(), calls=%async_computation.5 | async-start | bytes 1310720 | tf_op jit(solution)/shard_map/reduce_scatter | solution.py:120
  50.8 1.9 copy-start.5
  52.7 2.7 %copy-start.9 = (f32[192,256]{1,0:T(8,128)}, f32[192,256]{1,0:T(8,128)S(1)}, u32[]{:S(2)}) copy-start(f32[192,256]{1,0:T(8,128)S(1)} %fusion.45) | copy-start | bytes 589828
  52.7 1.2 copy-start.3
  53.9 1.5 copy-start.11
  53.9 1.6 copy-start.14
  53.9 29.6 %copy-start.7 = (s32[1,256,512]{2,1,0:T(8,128)S(1)}, s32[1,256,512]{2,1,0:T(8,128)}, u32[]{:S(2)}) copy-start(s32[1,256,512]{2,1,0:T(8,128)} %param.18) | copy-start | bytes 1572868
  53.9 29.6 %copy-start.8 = (f32[1,256,512]{2,1,0:T(8,128)S(1)}, f32[1,256,512]{2,1,0:T(8,128)}, u32[]{:S(2)}) copy-start(f32[1,256,512]{2,1,0:T(8,128)} %param.16) | copy-start | bytes 1572868
  55.4 31.2 %copy-start.2 = (bf16[1,192,2048]{2,1,0:T(8,128)(2,1)S(1)}, bf16[1,192,2048]{2,1,0:T(8,128)(2,1)}, u32[]{:S(2)}) copy-start(bf16[1,192,2048]{2,1,0:T(8,128)(2,1)} %param.11) | copy-start | bytes 2359300
  55.4 57.6 %all-gather.5.cloned.1.call-start = ((), (), s32[]{:S(2)}) async-start(), calls=%async_computation.3 | async-start | bytes 1310720 | tf_op jit(solution)/shard_map/all_gather | solution.py:76
  86.5 55.7 %all-reduce.3.cloned.1.call-start = ((), (), s32[]{:S(2)}) async-start(), calls=%async_computation.6 | async-start | bytes 3145728 | tf_op jit(solution)/shard_map/psum | solution.py:97
  86.8 26.2 %copy-start.10 = (f32[192,256]{1,0:T(8,128)S(1)}, f32[192,256]{1,0:T(8,128)}, u32[]{:S(2)}) copy-start(f32[192,256]{1,0:T(8,128)} %copy-done.9) | copy-start | bytes 589828
  86.8 26.2 %copy-start.12 = (f32[192,256]{1,0:T(8,128)S(1)}, f32[192,256]{1,0:T(8,128)}, u32[]{:S(2)}) copy-start(f32[192,256]{1,0:T(8,128)} %copy-done.11) | copy-start | bytes 589828
  118.3 1.9 copy-start.6
  121.6 59.8 %reduce-scatter.3.cloned.1.call-start = ((), (), s32[]{:S(2)}) async-start(), calls=%async_computation.4 | async-start | bytes 2621440 | tf_op jit(solution)/shard_map/reduce_scatter | solution.py:117
  142.2 5.2 %copy-start.4 = (bf16[192,2048]{1,0:T(8,128)(2,1)S(1)}, bf16[192,2048]{1,0:T(8,128)(2,1)}, u32[]{:S(2)}) copy-start(bf16[192,2048]{1,0:T(8,128)(2,1)} %get-tuple-element.5) | copy-start | bytes 2359300
  143.7 20.9 %collective-permute-start = (bf16[192,2048]{1,0:T(8,128)(2,1)S(1)}, bf16[192,2048]{1,0:T(8,128)(2,1)S(1)}, u32[]{:S(2)}, u32[]{:S(2)}) collective-permute-start(bf16[192,2048]{1,0:T(8,128)(2,1)S(1)} %fusion.10), channel_id=1, source_target_pairs={{0,8},{8,16},{16,24},{1,9},{9,17},{17,25},{2,10},{10,18},{18,26},{... | collective-permute-start | bytes 2359304 | tf_op jit(solution)/shard_map/ppermute | solution.py:18
  147.8 33.6 %copy-start.1 = (s32[1,2,512,256]{3,2,1,0:T(8,128)S(1)}, s32[1,2,512,256]{3,2,1,0:T(8,128)}, u32[]{:S(2)}) copy-start(s32[1,2,512,256]{3,2,1,0:T(8,128)} %param.17) | copy-start | bytes 3145732
  148.4 21.3 %collective-permute-start.1 = (bf16[192,2048]{1,0:T(8,128)(2,1)S(1)}, bf16[192,2048]{1,0:T(8,128)(2,1)S(1)}, u32[]{:S(2)}, u32[]{:S(2)}) collective-permute-start(bf16[192,2048]{1,0:T(8,128)(2,1)S(1)} %fusion.16), channel_id=1, source_target_pairs={{8,0},{16,8},{24,16},{9,1},{17,9},{25,17},{10,2},{18,10},{26,18},{... | collective-permute-start | bytes 2359304 | tf_op jit(solution)/shard_map/ppermute | solution.py:18
Sparse Core Ops, SparseCore 0:
  12.8 37.8 all-gather.2
  55.5 27.9 reduce-scatter.4
  86.6 26.3 all-gather.4
  121.7 20.4 all-reduce.2
  145.0 36.3 reduce-scatter.2
where the time goes:
time: 194 us
  waiting for transfers between devices  140 us (72%)
  other arithmetic  15.4 us (8%)
  matrix products  15.1 us (8%)
  between operations  14.6 us (8%)
  starting transfers between devices  5.21 us (3%)
  local copies, waits for them, and re-layouts  3.42 us (2%)
    all_gather x1, waiting for transfers between devices, local(): lax.all_gather(pred_in, 'dp', axis=1, tiled=True)  37.7 us
    reduce_scatter x1, waiting for transfers between devices, local(): lax.psum_scatter(local_out.astype(jnp.bfloat16), 'dp', scatter_dimension=...  28 us
    all_gather x1, waiting for transfers between devices, local(): lax.all_gather(pred_out, 'dp', axis=1, tiled=True)  24.5 us
    ppermute x2, waiting for transfers between devices, passed_along(): return lax.ppermute(block, axis, route)  20 us
    psum x1, waiting for transfers between devices, local(): lax.psum(partial_value.astype(jnp.bfloat16), 'hid').astype(jnp.float32)  17.8 us
    reduce_scatter x1, waiting for transfers between devices, local(): lax.psum_scatter(local_in.astype(jnp.bfloat16), 'dp', scatter_dimension=1...  11.7 us
    broadcast_in_dim x2, other arithmetic, local(): return (next_rows[None], back_rows[None], in_update[None], out_update[None])  6.92 us
    ppermute x2, starting transfers between devices, passed_along(): return lax.ppermute(block, axis, route)  5.01 us
  transfers between devices with their start and end apart: 7, of which 7 were waited for; matrix products, arithmetic and copies ran while one was open for 4% of the time, Pallas kernels for 0%

commit v1 on v0

--- a/solution.py
+++ b/solution.py
@@ -73,7 +73,7 @@
     )
     full_in, full_out = (
         lax.all_gather(pred_in, "dp", axis=1, tiled=True),
-        lax.all_gather(pred_out, "dp", axis=1, tiled=True),
+        jnp.concatenate(lax.all_gather(pred_out, "dp"), axis=1),
     )
     normed, factor, values = normalize(forward_input[0], gain)
     gate_val = jnp.dot(normed, full_in[0], preferred_element_type=jnp.float32)

time: 194 us -> 196 us (1.010)
  waiting for transfers between devices: 140 us -> 133 us
  local copies, waits for them, and re-layouts: 3.42 us -> 7.65 us
  other arithmetic: 15.4 us -> 19.3 us
    reduce_scatter x1, waiting for transfers between devices: 11.7 us -> 35.3 us  [local(): lax.psum_scatter(local_in.astype(jnp.bfloat16), 'dp', scatter_dimension=1...]
    ppermute x2, waiting for transfers between devices: 20 us -> 0.01 us  [passed_along(): return lax.ppermute(block, axis, route)]
    reduce_scatter x1, waiting for transfers between devices: 28 us -> 22.3 us  [local(): lax.psum_scatter(local_out.astype(jnp.bfloat16), 'dp', scatter_dimension=...]
    psum x1, waiting for transfers between devices: 17.8 us -> 15 us  [local(): lax.psum(partial_value.astype(jnp.bfloat16), 'hid').astype(jnp.float32)]
    convert_element_type x0 -> x1, other arithmetic: none -> 2.75 us  [local(): (out_weight[0] - LEARN_RATE * lag_value * direction(m_out, v_out, STEP -...]
    all_gather x1, waiting for transfers between devices: 37.7 us -> 35.4 us  [local(): lax.all_gather(pred_in, 'dp', axis=1, tiled=True)]
    all_gather x0 -> x1, local copies, waits for them, and re-layouts: none -> 2.26 us  [local(): lax.all_gather(pred_out, 'dp')]
    unnamed x33 -> x31, local copies, waits for them, and re-layouts: 2.71 us -> 4.61 us
  transfers between devices with their start and end apart: 7 -> 7, of which waited for: 7 -> 5; matrix products, arithmetic and copies ran while one was open for 4% -> 9% of each run, Pallas kernels for 0% -> 0%
where the time goes in v1:
time: 196 us
  waiting for transfers between devices  133 us (68%)
  other arithmetic  19.3 us (10%)
  matrix products  15 us (8%)
  between operations  14.6 us (7%)
  local copies, waits for them, and re-layouts  7.65 us (4%)
  starting transfers between devices  6.2 us (3%)
    all_gather x1, waiting for transfers between devices, local(): lax.all_gather(pred_in, 'dp', axis=1, tiled=True)  35.4 us
    reduce_scatter x1, waiting for transfers between devices, local(): lax.psum_scatter(local_in.astype(jnp.bfloat16), 'dp', scatter_dimension=1...  35.3 us
    all_gather x1, waiting for transfers between devices, local(): lax.all_gather(pred_out, 'dp')  24.8 us
    reduce_scatter x1, waiting for transfers between devices, local(): lax.psum_scatter(local_out.astype(jnp.bfloat16), 'dp', scatter_dimension=...  22.3 us
    psum x1, waiting for transfers between devices, local(): lax.psum(partial_value.astype(jnp.bfloat16), 'hid').astype(jnp.float32)  15 us
    broadcast_in_dim x2, other arithmetic, local(): return (next_rows[None], back_rows[None], in_update[None], out_update[None])  6.56 us
    ppermute x2, starting transfers between devices, passed_along(): return lax.ppermute(block, axis, route)  6 us
    unnamed x31, local copies, waits for them, and re-layouts  4.61 us
  transfers between devices with their start and end apart: 7, of which 5 were waited for; matrix products, arithmetic and copies ran while one was open for 9% of the time, Pallas kernels for 0%

profile of v1, /device:TPU:0, one launch (start us, length us, event | category | flops | bytes accessed | tf_op | source)
XLA Modules:
  0.0 195.6 jit_solution(12227045745335606454)
XLA Ops:
  7.2 0.0 all-gather.5.cloned.1.call-start
  7.2 0.8 fusion.108
  8.7 2.7 %subtract_convert_fusion = bf16[1,256,512]{2,1,0:T(8,128)(2,1)} fusion(f32[1,256,512]{2,1,0:T(8,128)} %param.16, s32[1,256,512]{2,1,0:T(8,128)} %param.18, f32[512]{0:T(512)S(1)} %bitcast.164, f32[512]{0:T(512)S(1)} %bitcast.162, f32[]{:T(128)} %bitcast.4), kind=kLoop, calls=%fused_computation.125 | loop fusion | flops 4456448 | bytes 1314820 | tf_op jit(solution)/shard_map/convert_element_type | solution.py:71
  11.4 0.0 all-gather.5.cloned.1.call-update
  11.4 0.0 all-gather.3.cloned.1.call-start
  11.5 0.0 copy-start.2
  11.5 0.0 copy-start
  11.6 3.8 %fusion.40 = bf16[2,512,256]{2,1,0:T(8,128)(2,1)} fusion(f32[1,2,512,256]{3,2,1,0:T(8,128)} %param.15, f32[]{:T(128)} %bitcast.4, s32[1,2,512,256]{3,2,1,0:T(8,128)S(1)} %copy-done.1, f32[2,512]{1,0:T(2,128)S(1)} %get-tuple-element.15, f32[2,512]{1,0:T(2,128)S(1)} %get-tuple-element.14), kind=kLoop, calls=%fused_computation.66 | loop fusion | flops 8912896 | bytes 2629636 | tf_op jit(solution)/shard_map/convert_element_type | solution.py:68
  15.4 0.0 all-gather.3.cloned.1.call-update
  15.4 0.0 all-reduce.3.cloned.1.call-start
  15.5 0.2 fusion.9
  15.7 0.2 fusion.13
  16.0 24.8 %all-gather.5.cloned.1.call-done = bf16[4,256,512]{2,1,0:T(8,128)(2,1)} async-done(((bf16[1,256,512]{2,1,0:T(8,128)(2,1)}), bf16[4,256,512]{2,1,0:T(8,128)(2,1)}) %all-gather.5.cloned.1.call-update) | async-done | bytes 1048592 | tf_op jit(solution)/shard_map/all_gather | solution.py:76
  40.8 2.3 %copy.20 = bf16[4,256,512]{1,2,0:T(8,128)(2,1)} copy(bf16[4,256,512]{2,1,0:T(8,128)(2,1)} %all-gather.5.cloned.1.call-done) | data formatting | bytes 2097152 | tf_op jit(solution)/shard_map/all_gather | solution.py:76
  43.1 35.4 %all-gather.3.cloned.1.call-done = bf16[2,2048,256]{2,1,0:T(8,128)(2,1)} async-done(((bf16[2,512,256]{2,1,0:T(8,128)(2,1)}), bf16[2,2048,256]{2,1,0:T(8,128)(2,1)}) %all-gather.3.cloned.1.call-update) | async-done | bytes 2097168 | tf_op jit(solution)/shard_map/all_gather | solution.py:75
  78.4 1.8 fusion.43
  80.3 0.1 copy-done.6
  80.4 0.4 fusion.45
  80.8 0.8 copy-done.3
  81.6 0.4 copy-done.8
  82.0 1.0 multiply_convert_fusion.1
  83.0 1.1 fusion.44
  84.1 3.7 %convolution_convert_fusion.3 = bf16[192,2048]{1,0:T(8,128)(2,1)} fusion(bf16[256,2048]{0,1:T(8,128)(2,1)} %bitcast.151, bf16[2,2048,256]{2,1,0:T(8,128)(2,1)} %all-gather.3.cloned.1.call-done, bf16[1,192,2048]{2,1,0:T(8,128)(2,1)S(1)} %copy-done.2, f32[2048]{0:T(1024)S(1)} %bitcast.157, f32[192]{0:T(256)S(1)} %add_rsqrt_fusion.1, f32[192,256]{1,0:T(8,128)} %fusion.44), kind=kOutput, calls=%fused_computation.5 | convolution fusion | flops 404914176 | bytes 3875584 | tf_op jit(solution)/shard_map/dot_general | solution.py:82
  87.8 1.9 fusion.42
  89.7 0.0 copy-done.7
  89.7 1.4 fusion
  91.1 0.0 all-reduce.3.cloned.1.call-update
  91.1 0.0 reduce-scatter.5.cloned.1.call-start
  91.2 2.5 %convolution_convert_fusion = bf16[256,2048]{1,0:T(8,128)(2,1)} fusion(bf16[1,192,2048]{2,1,0:T(8,128)(2,1)S(1)} %copy-done.3, f32[192,256]{1,0:T(8,128)} %copy-done.10, f32[192,256]{1,0:T(8,128)} %copy-done.9), kind=kOutput, calls=%fused_computation.1 | convolution fusion | flops 202145792 | bytes 2228224 | tf_op jit(solution)/shard_map/dot_general | solution.py:115
  93.7 0.0 reduce-scatter.5.cloned.1.call-update
  93.7 0.0 reduce-scatter.3.cloned.1.call-start
  93.7 0.6 fusion.2
  94.3 0.3 copy-done.11
  94.6 0.6 fusion.1
  95.2 1.5 pad_maximum_fusion
  96.7 0.0 reduce-scatter.3.cloned.1.call-update
  96.7 15.0 %all-reduce.3.cloned.1.call-done = (bf16[192,2048]{1,0:T(8,128)(2,1)}, bf16[192,2048]{1,0:T(8,128)(2,1)}) async-done(((bf16[192,2048]{1,0:T(8,128)(2,1)}, bf16[192,2048]{1,0:T(8,128)(2,1)}), (bf16[192,2048]{1,0:T(8,128)(2,1)}, bf16[192,2048]{1,0:T(8,128)(2,1)})) %all-reduce.3.cloned.1.call-update) | async-done | bytes 1572880 | tf_op jit(solution)/shard_map/psum | solution.py:97
  111.7 2.4 %fusion.10 = bf16[192,2048]{1,0:T(8,128)(2,1)} fusion(bf16[1,192,2048]{2,1,0:T(8,128)(2,1)S(1)} %copy-done.2, bf16[192,2048]{1,0:T(8,128)(2,1)} %get-tuple-element.4), kind=kLoop, calls=%fused_computation.20 | loop fusion | flops 1572864 | bytes 2359296 | tf_op jit(solution)/shard_map/convert_element_type | solution.py:100
  114.1 4.5 %collective-permute-start = (bf16[192,2048]{1,0:T(8,128)(2,1)}, bf16[192,2048]{1,0:T(8,128)(2,1)}, u32[]{:S(2)}, u32[]{:S(2)}) collective-permute-start(bf16[192,2048]{1,0:T(8,128)(2,1)} %fusion.10), channel_id=1, source_target_pairs={{0,8},{8,16},{16,24},{1,9},{9,17},{17,25},{2,10},{10,18},{18,26},{... | collective-permute-start | bytes 2359304 | tf_op jit(solution)/shard_map/ppermute | solution.py:18
  118.6 0.3 fusion.17
  119.0 1.5 fusion.16
  120.5 1.5 collective-permute-start.1
  121.9 22.3 %reduce-scatter.5.cloned.1.call-done = bf16[256,512]{1,0:T(8,128)(2,1)} async-done(((bf16[256,2048]{1,0:T(8,128)(2,1)}), bf16[256,512]{1,0:T(8,128)(2,1)}) %reduce-scatter.5.cloned.1.call-update) | async-done | bytes 262160 | tf_op jit(solution)/shard_map/reduce_scatter | solution.py:120
  144.2 2.7 %fusion.86 = f32[1,256,512]{2,1,0:T(8,128)} fusion(bf16[256,512]{1,0:T(8,128)(2,1)} %reduce-scatter.5.cloned.1.call-done, s32[1,256,512]{2,1,0:T(8,128)S(1)} %copy-done.5, f32[512]{0:T(512)S(1)} %bitcast.165, f32[512]{0:T(512)S(1)} %bitcast.163), kind=kLoop, calls=%fused_computation.129 | loop fusion | flops 5111808 | bytes 1314816 | tf_op jit(solution)/shard_map/broadcast_in_dim | solution.py:133
  146.9 35.3 %reduce-scatter.3.cloned.1.call-done = bf16[2,512,256]{2,1,0:T(8,128)(2,1)} async-done(((bf16[2,2048,256]{2,1,0:T(8,128)(2,1)}), bf16[2,512,256]{2,1,0:T(8,128)(2,1)}) %reduce-scatter.3.cloned.1.call-update) | async-done | bytes 524304 | tf_op jit(solution)/shard_map/reduce_scatter | solution.py:117
  182.2 3.9 %fusion.33 = f32[1,2,512,256]{3,2,1,0:T(8,128)} fusion(bf16[2,512,256]{2,1,0:T(8,128)(2,1)} %reduce-scatter.3.cloned.1.call-done, s32[1,2,512,256]{3,2,1,0:T(8,128)S(1)} %copy-done.1, f32[2,512]{1,0:T(2,128)S(1)} %get-tuple-element.15, f32[2,512]{1,0:T(2,128)S(1)} %get-tuple-element.14), kind=kLoop, calls=%fused_computation.54 | loop fusion | flops 10223616 | bytes 2629632 | tf_op jit(solution)/shard_map/broadcast_in_dim | solution.py:133
  186.1 2.1 %copy.30 = bf16[1,192,2048]{2,1,0:T(8,128)(2,1)} copy(bf16[1,192,2048]{2,1,0:T(8,128)(2,1)} %bitcast.12) | data formatting | bytes 1572864
  188.2 0.9 copy.31
  (28 shorter events, 0.1 us)
Async XLA Ops:
  7.2 4.3 %copy-start.13 = (f32[1,2,2,512,1]{3,4,2,1,0:T(1,128)S(1)}, f32[1,2,2,512,1]{3,4,2,1,0:T(1,128)}, u32[]{:S(2)}) copy-start(f32[1,2,2,512,1]{3,4,2,1,0:T(1,128)} %param.19) | copy-start | bytes 24580
  7.2 4.4 %copy-start.1 = (s32[1,2,512,256]{3,2,1,0:T(8,128)S(1)}, s32[1,2,512,256]{3,2,1,0:T(8,128)}, u32[]{:S(2)}) copy-start(s32[1,2,512,256]{3,2,1,0:T(8,128)} %param.17) | copy-start | bytes 3145732
  7.2 33.6 %all-gather.5.cloned.1.call-start = ((), (), s32[]{:S(2)}) async-start(), calls=%async_computation.3 | async-start | bytes 1310720 | tf_op jit(solution)/shard_map/all_gather | solution.py:76
  11.4 67.0 %all-gather.3.cloned.1.call-start = ((), (), s32[]{:S(2)}) async-start(), calls=%async_computation.2 | async-start | bytes 2621440 | tf_op jit(solution)/shard_map/all_gather | solution.py:75
  11.5 3.9 %copy-start.2 = (bf16[1,192,2048]{2,1,0:T(8,128)(2,1)S(1)}, bf16[1,192,2048]{2,1,0:T(8,128)(2,1)}, u32[]{:S(2)}) copy-start(bf16[1,192,2048]{2,1,0:T(8,128)(2,1)} %param.11) | copy-start | bytes 2359300
  11.5 4.2 %copy-start = (bf16[1,192,2048]{2,1,0:T(8,128)(2,1)S(1)}, bf16[1,192,2048]{2,1,0:T(8,128)(2,1)}, u32[]{:S(2)}) copy-start(bf16[1,192,2048]{2,1,0:T(8,128)(2,1)} %param.12) | copy-start | bytes 2359300
  15.4 96.3 %all-reduce.3.cloned.1.call-start = ((), (), s32[]{:S(2)}) async-start(), calls=%async_computation.6 | async-start | bytes 3145728 | tf_op jit(solution)/shard_map/psum | solution.py:97
  15.7 62.7 %copy-start.12 = (f32[1,2048]{1,0:T(1,128)S(1)}, f32[1,2048]{1,0:T(1,128)}, u32[]{:S(2)}) copy-start(f32[1,2048]{1,0:T(1,128)} %param.14) | copy-start | bytes 24580
  78.4 1.9 copy-start.6
  80.4 2.6 %copy-start.9 = (f32[192,256]{1,0:T(8,128)}, f32[192,256]{1,0:T(8,128)S(1)}, u32[]{:S(2)}) copy-start(f32[192,256]{1,0:T(8,128)S(1)} %fusion.43) | copy-start | bytes 589828
  80.4 1.2 copy-start.3
  80.4 1.6 copy-start.8
  80.8 2.2 %copy-start.10 = (f32[192,256]{1,0:T(8,128)}, f32[192,256]{1,0:T(8,128)S(1)}, u32[]{:S(2)}) copy-start(f32[192,256]{1,0:T(8,128)S(1)} %fusion.45) | copy-start | bytes 589828
  87.8 2.0 copy-start.7
  91.1 53.1 %reduce-scatter.5.cloned.1.call-start = ((), (), s32[]{:S(2)}) async-start(), calls=%async_computation.5 | async-start | bytes 1310720 | tf_op jit(solution)/shard_map/reduce_scatter | solution.py:120
  93.7 88.6 %reduce-scatter.3.cloned.1.call-start = ((), (), s32[]{:S(2)}) async-start(), calls=%async_computation.4 | async-start | bytes 2621440 | tf_op jit(solution)/shard_map/reduce_scatter | solution.py:117
  93.7 0.9 copy-start.11
  111.7 6.9 %copy-start.4 = (bf16[192,2048]{1,0:T(8,128)(2,1)S(1)}, bf16[192,2048]{1,0:T(8,128)(2,1)}, u32[]{:S(2)}) copy-start(bf16[192,2048]{1,0:T(8,128)(2,1)} %get-tuple-element.5) | copy-start | bytes 2359300
  114.1 32.8 %collective-permute-start = (bf16[192,2048]{1,0:T(8,128)(2,1)}, bf16[192,2048]{1,0:T(8,128)(2,1)}, u32[]{:S(2)}, u32[]{:S(2)}) collective-permute-start(bf16[192,2048]{1,0:T(8,128)(2,1)} %fusion.10), channel_id=1, source_target_pairs={{0,8},{8,16},{16,24},{1,9},{9,17},{17,25},{2,10},{10,18},{18,26},{... | collective-permute-start | bytes 2359304 | tf_op jit(solution)/shard_map/ppermute | solution.py:18
  119.0 25.2 %copy-start.5 = (s32[1,256,512]{2,1,0:T(8,128)S(1)}, s32[1,256,512]{2,1,0:T(8,128)}, u32[]{:S(2)}) copy-start(s32[1,256,512]{2,1,0:T(8,128)} %param.18) | copy-start | bytes 1572868
  120.5 26.4 %collective-permute-start.1 = (bf16[192,2048]{1,0:T(8,128)(2,1)}, bf16[192,2048]{1,0:T(8,128)(2,1)S(1)}, u32[]{:S(2)}, u32[]{:S(2)}) collective-permute-start(bf16[192,2048]{1,0:T(8,128)(2,1)} %fusion.16), channel_id=1, source_target_pairs={{8,0},{16,8},{24,16},{9,1},{17,9},{25,17},{10,2},{18,10},{26,18},{... | collective-permute-start | bytes 2359304 | tf_op jit(solution)/shard_map/ppermute | solution.py:18
Sparse Core Ops, SparseCore 0:
  11.6 29.2 all-gather.4
  43.2 35.1 all-gather.2
  91.3 20.4 all-reduce.2
  115.0 29.1 reduce-scatter.4
  147.0 35.1 reduce-scatter.2
